TPU v7x, 32 devices: a whole 2x2x4 slice. The times are simulated.
32 devices in a mesh: row: 8 (over y, x, core), col: 4 (over z).
Axes of the slice: x: 2, y: 2, z: 4, core: 2. Of those that a mesh axis runs over, the one named last changes fastest.
Arguments:
- matrix: float32 [5120, 5120], P('row', 'col'), may hold values from -64 to 64
Outputs:
- iterate: float32 [5120, 5120], P('row', 'col')
- trace_value: float32 [2], replicated
- frobenius: float32 [2], replicated
All inputs are finite; a program needn't handle non-finite values.
Results may differ from a plain program's by a relative error of at most 0.003.
Values may be sent and summed in bfloat16 or wider, within the bound.
A program may use at most 64 MiB of HBM per device.

v0:
```python
import jax
import jax.numpy as jnp
from jax import lax
from jax.sharding import PartitionSpec as P

ITERS = 2
target = 0.0625


def add_columns(portion, left_panel):
    return jnp.dot(left_panel, portion, preferred_element_type=jnp.float32)


def on_device(matrix):
    rounded = matrix.astype(jnp.bfloat16)
    current = rounded.astype(jnp.float32)
    row_ids = lax.axis_index("row") * matrix.shape[0] + lax.broadcasted_iota(
        jnp.int32, matrix.shape, 0
    )
    col_ids = lax.axis_index("col") * matrix.shape[1] + lax.broadcasted_iota(
        jnp.int32, matrix.shape, 1
    )
    on_diagonal = row_ids == col_ids
    traces = []
    norms = []
    for step in range(ITERS):
        row_panel = lax.all_gather(rounded, "col", axis=1, tiled=True)
        if step == 0:
            order_full = row_panel.shape[1]
            squares = lax.psum(jnp.sum(current * current), ("row", "col"))
            scale = target * order_full / (squares + 1e-06)
            root = jnp.sqrt(scale)
        else:
            scale = jnp.float32(1.0)
            root = jnp.float32(1.0)
        product = add_columns(
            lax.all_gather(rounded, "row", axis=0, tiled=True), left_panel=row_panel
        )
        squared = (product * scale).astype(jnp.bfloat16)
        cubic_part = add_columns(
            lax.all_gather(squared, "row", axis=0, tiled=True), left_panel=row_panel
        )
        current = root * (1.5 * current - 0.5 * cubic_part)
        rounded = current.astype(jnp.bfloat16)
        diagonal_part = jnp.sum(jnp.where(on_diagonal, current, 0.0))
        square_part = jnp.sum(current * current)
        trace_now, total_now = lax.psum((diagonal_part, square_part), ("row", "col"))
        traces.append(trace_now)
        norms.append(jnp.sqrt(total_now))
    return (current, jnp.stack(traces), jnp.stack(norms))


def solution(mesh):
    in_specs = (P("row", "col"),)
    out_specs = (P("row", "col"), P(), P())
    return jax.shard_map(
        on_device, mesh=mesh, in_specs=in_specs, out_specs=out_specs, check_vma=False
    )
```

profile of v0, /device:TPU:0, one launch (start us, length us, event | category | flops | bytes accessed | tf_op | source)
XLA Modules:
  0.0 667.8 jit_solution(10903226945213668132)
XLA Ops:
  7.2 0.0 all-gather.7.cloned.1.call-start
  7.2 4.0 copy.4
  11.2 0.0 copy-start
  11.2 0.0 all-gather.7.cloned.1.call-update
  11.2 0.0 all-gather.9.cloned.1.call-start
  11.3 0.7 all-gather.9.cloned.1.call-update
  12.0 0.0 all-gather.11.cloned.1.call-start
  12.0 0.6 copy-done
  12.6 1.4 fusion.4
  14.1 51.2 %psum.35 = f32[]{:T(128)} all-reduce(f32[]{:T(128)} %fusion.4), channel_id=1, replica_groups=mesh['row'=8,'col'=4] {'row','col'}, use_global_device_ids=true, to_apply=%region_1.0 | all-reduce | flops 1 | bytes 8 | tf_op jit(solution)/shard_map/psum | solution.py:30
  65.9 68.8 %all-gather.7.cloned.1.call-done = bf16[640,5120]{0,1:T(8,128)(2,1)} async-done(((bf16[640,1280]{0,1:T(8,128)(2,1)}), bf16[640,5120]{0,1:T(8,128)(2,1)}) %all-gather.7.cloned.1.call-update) | async-done | bytes 6553616 | tf_op jit(solution)/shard_map/all_gather | solution.py:27
  134.8 74.7 %all-gather.9.cloned.1.call-done = bf16[5120,1280]{0,1:T(8,128)(2,1)} async-done(((bf16[640,1280]{0,1:T(8,128)(2,1)}), bf16[5120,1280]{0,1:T(8,128)(2,1)}) %all-gather.9.cloned.1.call-update) | async-done | bytes 13107216 | tf_op jit(solution)/shard_map/all_gather | solution.py:37
  209.4 14.1 %fusion.7 = bf16[640,1280]{1,0:T(8,128)(2,1)} fusion(bf16[640,5120]{0,1:T(8,128)(2,1)} %all-gather.7.cloned.1.call-done, bf16[5120,1280]{0,1:T(8,128)(2,1)} %all-gather.9.cloned.1.call-done, f32[]{:T(128)S(6)} %div.3), kind=kOutput, calls=%fused_computation.16 | convolution fusion | flops 8390246400 | bytes 21299204 | tf_op jit(solution)/shard_map/dot_general | solution.py:11
  223.5 0.0 all-gather.11.cloned.1.call-update
  223.6 0.0 all-gather.13.cloned.1.call-start
  223.7 74.2 %all-gather.11.cloned.1.call-done = bf16[5120,1280]{1,0:T(8,128)(2,1)} async-done(((bf16[640,1280]{1,0:T(8,128)(2,1)}), bf16[5120,1280]{1,0:T(8,128)(2,1)}) %all-gather.11.cloned.1.call-update) | async-done | bytes 13107216 | tf_op jit(solution)/shard_map/all_gather | solution.py:41
  297.9 18.0 %multiply_reduce_fusion.1 = (f32[]{:T(128)}, f32[]{:T(128)}, bf16[640,1280]{0,1:T(8,128)(2,1)}, f32[640,1280]{0,1:T(8,128)}) fusion(s32[1280]{0:T(1024)S(1)} %iota_add_fusion, s32[640]{0:T(1024)S(1)} %iota_add_fusion.1, bf16[5120,1280]{1,0:T(8,128)(2,1)} %all-gather.11.cloned.1.call-done, bf16[640,5120]{0,1:T(8,128)(2,1)} %all-gather.7.cloned.1.call-done, ...), kind=kOutput, calls=%fused_computation.15 | convolution fusion | flops 8397619200 | bytes 26222092 | tf_op jit(solution)/shard_map/dot_general | solution.py:11
  315.9 0.0 all-gather.13.cloned.1.call-update
  316.0 0.0 all-gather.15.cloned.1.call-start
  316.0 0.5 all-gather.15.cloned.1.call-update
  316.6 0.2 all-gather.17.cloned.1.call-start
  316.8 118.9 %all-gather.13.cloned.1.call-done = bf16[640,5120]{0,1:T(8,128)(2,1)} async-done(((bf16[640,1280]{0,1:T(8,128)(2,1)}), bf16[640,5120]{0,1:T(8,128)(2,1)}) %all-gather.13.cloned.1.call-update) | async-done | bytes 6553616 | tf_op jit(solution)/shard_map/all_gather | solution.py:27
  435.7 74.0 %all-gather.15.cloned.1.call-done = bf16[5120,1280]{0,1:T(8,128)(2,1)} async-done(((bf16[640,1280]{0,1:T(8,128)(2,1)}), bf16[5120,1280]{0,1:T(8,128)(2,1)}) %all-gather.15.cloned.1.call-update) | async-done | bytes 13107216 | tf_op jit(solution)/shard_map/all_gather | solution.py:37
  509.7 14.1 %convolution_convert_fusion = bf16[640,1280]{1,0:T(8,128)(2,1)} fusion(bf16[640,5120]{0,1:T(8,128)(2,1)} %all-gather.13.cloned.1.call-done, bf16[5120,1280]{0,1:T(8,128)(2,1)} %all-gather.15.cloned.1.call-done), kind=kOutput, calls=%fused_computation.17 | convolution fusion | flops 8389427200 | bytes 21299200 | tf_op jit(solution)/shard_map/dot_general | solution.py:11
  523.8 0.0 all-gather.17.cloned.1.call-update
  523.8 74.4 %all-gather.17.cloned.1.call-done = bf16[5120,1280]{1,0:T(8,128)(2,1)} async-done(((bf16[640,1280]{1,0:T(8,128)(2,1)}), bf16[5120,1280]{1,0:T(8,128)(2,1)}) %all-gather.17.cloned.1.call-update) | async-done | bytes 13107216 | tf_op jit(solution)/shard_map/all_gather | solution.py:41
  598.2 17.0 %multiply_reduce_fusion = (f32[]{:T(128)}, f32[]{:T(128)}, f32[640,1280]{0,1:T(8,128)S(1)}) fusion(s32[1280]{0:T(1024)S(1)} %iota_add_fusion, s32[640]{0:T(1024)S(1)} %iota_add_fusion.1, bf16[640,5120]{0,1:T(8,128)(2,1)} %all-gather.13.cloned.1.call-done, bf16[5120,1280]{1,0:T(8,128)(2,1)} %all-gather.17.cloned.1.call-done, f32[640,1280]{0,1:T(8,128)} %get-tuple-element.15), kind=kOutput, calls=%fused_computation.14 | convolution fusion | flops 8395161600 | bytes 26222088 | tf_op jit(solution)/shard_map/dot_general | solution.py:11
  615.2 2.9 copy.6
  618.1 39.6 %all-reduce = (f32[1]{0:T(128)}, f32[1]{0:T(128)}, f32[]{:T(128)}, f32[]{:T(128)}) all-reduce(f32[1]{0:T(128)} %bitcast.2, f32[1]{0:T(128)} %bitcast.1, f32[]{:T(128)} %get-tuple-element.8, f32[]{:T(128)} %get-tuple-element.6), channel_id=1, replica_groups=mesh['row'=8,'col'=4] {'row','col'}, use_global_device_ids=true, to_apply=%region_5.6 | all-reduce | flops 4 | bytes 32 | tf_op jit(solution)/shard_map/psum | solution.py:47
  659.1 1.8 pad_maximum_fusion
  (2 shorter events, 0.0 us)
Async XLA Ops:
  7.2 127.6 %all-gather.7.cloned.1.call-start = ((), (), s32[]{:S(2)}) async-start(), calls=%async_computation | async-start | bytes 8192000 | tf_op jit(solution)/shard_map/all_gather | solution.py:27
  11.2 1.4 copy-start
  11.2 198.2 %all-gather.9.cloned.1.call-start = ((), (), s32[]{:S(2)}) async-start(), calls=%async_computation.1 | async-start | bytes 14745600 | tf_op jit(solution)/shard_map/all_gather | solution.py:37
  12.0 286.0 %all-gather.11.cloned.1.call-start = ((), (), s32[]{:S(2)}) async-start(), calls=%async_computation.2 | async-start | bytes 14745600 | tf_op jit(solution)/shard_map/all_gather | solution.py:41
  223.6 212.2 %all-gather.13.cloned.1.call-start = ((), (), s32[]{:S(2)}) async-start(), calls=%async_computation.3 | async-start | bytes 8192000 | tf_op jit(solution)/shard_map/all_gather | solution.py:27
  316.0 193.8 %all-gather.15.cloned.1.call-start = ((), (), s32[]{:S(2)}) async-start(), calls=%async_computation.4 | async-start | bytes 14745600 | tf_op jit(solution)/shard_map/all_gather | solution.py:37
  316.6 281.6 %all-gather.17.cloned.1.call-start = ((), (), s32[]{:S(2)}) async-start(), calls=%async_computation.5 | async-start | bytes 14745600 | tf_op jit(solution)/shard_map/all_gather | solution.py:41
Sparse Core Ops, SparseCore 0:
  11.3 123.3 all-gather.6
  137.2 72.1 all-gather.8
  223.7 74.1 all-gather.10
  316.1 119.5 all-gather.12
  437.5 72.2 all-gather.14
  524.0 74.1 all-gather.16
where the time goes:
time: 668 us
  waiting for transfers between devices  486 us (73%)
  blocking collectives  90.8 us (14%)
  matrix products  63.2 us (9%)
  between operations  16.2 us (2%)
  local copies, waits for them, and re-layouts  7.52 us (1%)
    all_gather x2, waiting for transfers between devices, on_device(): row_panel = lax.all_gather(rounded, 'col', axis=1, tiled=True)  188 us
    all_gather x2, waiting for transfers between devices, on_device(): lax.all_gather(rounded, 'row', axis=0, tiled=True)  149 us
    all_gather x2, waiting for transfers between devices, on_device(): lax.all_gather(squared, 'row', axis=0, tiled=True)  149 us
    dot_general x4, matrix products, add_columns(): return jnp.dot(left_panel, portion, preferred_element_type=jnp.float32)  63.2 us
    psum x1, blocking collectives, on_device(): squares = lax.psum(jnp.sum(current * current), ('row', 'col'))  51.2 us
    psum x1, blocking collectives, on_device(): lax.psum((diagonal_part, square_part), ('row', 'col'))  39.6 us
  transfers between devices with their start and end apart: 6, of which 6 were waited for; matrix products, arithmetic and copies ran while one was open for 0% of the time, Pallas kernels for 0%

commit v1 on v0

--- a/solution.py
+++ b/solution.py
@@ -24,7 +24,14 @@
     traces = []
     norms = []
     for step in range(ITERS):
-        row_panel = lax.all_gather(rounded, "col", axis=1, tiled=True)
+        ring = [rounded]
+        for hop in range(3):
+            ring.append(lax.ppermute(ring[-1], "col", [(dev, (dev + 1) % 4) for dev in range(4)]))
+        row_panel = jnp.roll(
+            jnp.concatenate(ring[::-1], axis=1),
+            (lax.axis_index("col") + 1) * ring[0].shape[1],
+            axis=1,
+        )
         if step == 0:
             order_full = row_panel.shape[1]
             squares = lax.psum(jnp.sum(current * current), ("row", "col"))

time: 668 us -> 568 us (0.85)
  waiting for transfers between devices: 486 us -> 338 us
  other arithmetic: 3.28 us -> 50 us
  local copies, waits for them, and re-layouts: 7.52 us -> 0.01 us
    ppermute x0 -> x6, waiting for transfers between devices: none -> 192 us  [on_device(): lax.ppermute(ring[-1], 'col', [(dev, (dev + 1) % 4) for dev in range(4)])]
    all_gather x2 -> x0, waiting for transfers between devices: 188 us -> none  [on_device(): row_panel = lax.all_gather(rounded, 'col', axis=1, tiled=True)]
    all_gather x2, waiting for transfers between devices: 149 us -> 0.01 us  [on_device(): lax.all_gather(rounded, 'row', axis=0, tiled=True)]
    concatenate x0 -> x2, other arithmetic: none -> 43.7 us  [on_device(): jnp.roll(jnp.concatenate(ring[::-1], axis=1), (lax.axis_index('col') + 1)...]
    unnamed x4, local copies, waits for them, and re-layouts: 7.52 us -> 0.01 us
  transfers between devices with their start and end apart: 6 -> 10, of which waited for: 6 -> 7; matrix products, arithmetic and copies ran while one was open for 0% -> 8% of each run, Pallas kernels for 0% -> 0%
where the time goes in v1:
time: 568 us
  waiting for transfers between devices  338 us (60%)
  blocking collectives  97.4 us (17%)
  matrix products  61.6 us (11%)
  other arithmetic  50 us (9%)
  between operations  16 us (3%)
    ppermute x6, waiting for transfers between devices, on_device(): lax.ppermute(ring[-1], 'col', [(dev, (dev + 1) % 4) for dev in range(4)])  192 us
    all_gather x2, waiting for transfers between devices, on_device(): lax.all_gather(squared, 'row', axis=0, tiled=True)  146 us
    dot_general x4, matrix products, add_columns(): return jnp.dot(left_panel, portion, preferred_element_type=jnp.float32)  61.6 us
    psum x1, blocking collectives, on_device(): squares = lax.psum(jnp.sum(current * current), ('row', 'col'))  57.8 us
    concatenate x2, other arithmetic, on_device(): jnp.roll(jnp.concatenate(ring[::-1], axis=1), (lax.axis_index('col') + 1)...  43.7 us
    psum x1, blocking collectives, on_device(): lax.psum((diagonal_part, square_part), ('row', 'col'))  39.6 us
  transfers between devices with their start and end apart: 10, of which 7 were waited for; matrix products, arithmetic and copies ran while one was open for 8% of the time, Pallas kernels for 0%

profile of v1, /device:TPU:0, one launch (start us, length us, event | category | flops | bytes accessed | tf_op | source)
XLA Modules:
  0.0 568.0 jit_solution(3937116264766120435)
XLA Ops:
  7.2 0.0 all-gather.5.cloned.1.call-start
  7.2 4.5 fusion.16
  11.7 0.0 all-gather.5.cloned.1.call-update
  11.7 0.0 all-gather.7.cloned.1.call-start
  11.7 3.1 collective-permute-start
  14.8 38.0 %collective-permute-done = bf16[640,1280]{1,0:T(8,128)(2,1)S(1)} collective-permute-done((bf16[640,1280]{1,0:T(8,128)(2,1)}, bf16[640,1280]{1,0:T(8,128)(2,1)S(1)}, u32[]{:S(2)}, u32[]{:S(2)}) %collective-permute-start) | collective-permute-done | bytes 1638432 | tf_op jit(solution)/shard_map/ppermute | solution.py:29
  52.9 0.0 collective-permute-start.1
  52.9 38.8 %collective-permute-done.1 = bf16[640,1280]{1,0:T(8,128)(2,1)S(1)} collective-permute-done((bf16[640,1280]{1,0:T(8,128)(2,1)S(1)}, bf16[640,1280]{1,0:T(8,128)(2,1)S(1)}, u32[]{:S(2)}, u32[]{:S(2)}) %collective-permute-start.1) | collective-permute-done | bytes 1638432 | tf_op jit(solution)/shard_map/ppermute | solution.py:29
  91.6 0.0 collective-permute-start.2
  91.6 57.8 %psum.35 = f32[]{:T(128)} all-reduce(f32[]{:T(128)} %get-tuple-element.12), channel_id=1, replica_groups=mesh['row'=8,'col'=4] {'row','col'}, use_global_device_ids=true, to_apply=%region_1.2 | all-reduce | flops 1 | bytes 8 | tf_op jit(solution)/shard_map/psum | solution.py:37
  150.1 0.0 collective-permute-done.2
  150.1 21.9 %fusion.10 = bf16[640,5120]{1,0:T(8,128)(2,1)} fusion(s32[]{:T(128)S(6)} %select_n.22, bf16[640,1280]{1,0:T(8,128)(2,1)} %collective-permute-done.2, bf16[640,1280]{1,0:T(8,128)(2,1)S(1)} %collective-permute-done.1, bf16[640,1280]{1,0:T(8,128)(2,1)S(1)} %collective-permute-done, bf16[640,1280]{1,0:T(8,128)(2,1)} %get-tuple-element.13), kind=kLoop, calls=%fused_computation.26 | loop fusion | flops 52428800 | bytes 13107204 | tf_op jit(solution)/shard_map/jit(_roll_dynamic)/concatenate | solution.py:30
  172.1 0.0 copy-start
  172.1 0.0 all-gather.5.cloned.1.call-done
  172.1 14.1 %fusion.19 = bf16[640,1280]{1,0:T(8,128)(2,1)} fusion(bf16[640,5120]{1,0:T(8,128)(2,1)} %fusion.10, bf16[5120,1280]{1,0:T(8,128)(2,1)} %all-gather.5.cloned.1.call-done, f32[]{:T(128)S(6)} %div.3), kind=kOutput, calls=%fused_computation.45 | convolution fusion | flops 8390246400 | bytes 21299204 | tf_op jit(solution)/shard_map/dot_general | solution.py:11
  186.2 0.0 all-gather.7.cloned.1.call-update
  186.2 0.2 all-gather.9.cloned.1.call-start
  186.5 74.1 %all-gather.7.cloned.1.call-done = bf16[5120,1280]{1,0:T(8,128)(2,1)} async-done(((bf16[640,1280]{1,0:T(8,128)(2,1)}), bf16[5120,1280]{1,0:T(8,128)(2,1)}) %all-gather.7.cloned.1.call-update) | async-done | bytes 13107216 | tf_op jit(solution)/shard_map/all_gather | solution.py:48
  260.6 0.0 copy-done
  260.6 16.9 %multiply_reduce_fusion.1 = (f32[]{:T(128)}, f32[]{:T(128)}, bf16[640,1280]{1,0:T(8,128)(2,1)}, f32[640,1280]{1,0:T(8,128)}) fusion(s32[1280]{0:T(1024)S(1)} %iota_add_fusion, s32[640]{0:T(1024)S(1)} %iota_add_fusion.1, bf16[640,5120]{1,0:T(8,128)(2,1)} %fusion.10, bf16[5120,1280]{1,0:T(8,128)(2,1)} %all-gather.7.cloned.1.call-done, ...), kind=kOutput, calls=%fused_computation.43 | convolution fusion | flops 8397619200 | bytes 26222092 | tf_op jit(solution)/shard_map/dot_general | solution.py:11
  277.5 0.0 all-gather.9.cloned.1.call-update
  277.5 0.0 all-gather.11.cloned.1.call-start
  277.6 1.5 collective-permute-start.3
  279.1 38.5 %collective-permute-done.3 = bf16[640,1280]{1,0:T(8,128)(2,1)S(1)} collective-permute-done((bf16[640,1280]{1,0:T(8,128)(2,1)}, bf16[640,1280]{1,0:T(8,128)(2,1)S(1)}, u32[]{:S(2)}, u32[]{:S(2)}) %collective-permute-start.3) | collective-permute-done | bytes 1638432 | tf_op jit(solution)/shard_map/ppermute | solution.py:29
  317.6 0.0 collective-permute-start.4
  317.6 38.9 %collective-permute-done.4 = bf16[640,1280]{1,0:T(8,128)(2,1)S(1)} collective-permute-done((bf16[640,1280]{1,0:T(8,128)(2,1)S(1)}, bf16[640,1280]{1,0:T(8,128)(2,1)S(1)}, u32[]{:S(2)}, u32[]{:S(2)}) %collective-permute-start.4) | collective-permute-done | bytes 1638432 | tf_op jit(solution)/shard_map/ppermute | solution.py:29
  356.5 0.0 collective-permute-start.5
  356.5 38.0 %collective-permute-done.5 = bf16[640,1280]{1,0:T(8,128)(2,1)S(1)} collective-permute-done((bf16[640,1280]{1,0:T(8,128)(2,1)S(1)}, bf16[640,1280]{1,0:T(8,128)(2,1)S(1)}, u32[]{:S(2)}, u32[]{:S(2)}) %collective-permute-start.5) | collective-permute-done | bytes 1638432 | tf_op jit(solution)/shard_map/ppermute | solution.py:29
  394.5 21.8 %fusion.3 = bf16[640,5120]{1,0:T(8,128)(2,1)} fusion(s32[]{:T(128)S(6)} %select_n.22, bf16[640,1280]{1,0:T(8,128)(2,1)S(1)} %collective-permute-done.5, bf16[640,1280]{1,0:T(8,128)(2,1)S(1)} %collective-permute-done.4, bf16[640,1280]{1,0:T(8,128)(2,1)S(1)} %collective-permute-done.3, bf16[640,1280]{1,0:T(8,128)(2,1)} %get-tuple-element.14), kind=kLoop, calls=%fused_computation.19 | loop fusion | flops 52428800 | bytes 13107204 | tf_op jit(solution)/shard_map/jit(_roll_dynamic)/concatenate | solution.py:30
  416.3 0.0 copy-start.1
  416.3 0.0 all-gather.9.cloned.1.call-done
  416.3 14.1 %convolution_convert_fusion = bf16[640,1280]{1,0:T(8,128)(2,1)} fusion(bf16[640,5120]{1,0:T(8,128)(2,1)} %fusion.3, bf16[5120,1280]{1,0:T(8,128)(2,1)} %all-gather.9.cloned.1.call-done), kind=kOutput, calls=%fused_computation.46 | convolution fusion | flops 8389427200 | bytes 21299200 | tf_op jit(solution)/shard_map/dot_general | solution.py:11
  430.5 0.0 all-gather.11.cloned.1.call-update
  430.5 71.6 %all-gather.11.cloned.1.call-done = bf16[5120,1280]{1,0:T(8,128)(2,1)} async-done(((bf16[640,1280]{1,0:T(8,128)(2,1)}), bf16[5120,1280]{1,0:T(8,128)(2,1)}) %all-gather.11.cloned.1.call-update) | async-done | bytes 13107216 | tf_op jit(solution)/shard_map/all_gather | solution.py:48
  502.1 0.0 copy-done.1
  502.1 16.5 %multiply_reduce_fusion = (f32[]{:T(128)}, f32[]{:T(128)}, f32[640,1280]{1,0:T(8,128)}) fusion(s32[1280]{0:T(1024)S(1)} %iota_add_fusion, s32[640]{0:T(1024)S(1)} %iota_add_fusion.1, bf16[640,5120]{1,0:T(8,128)(2,1)} %fusion.3, bf16[5120,1280]{1,0:T(8,128)(2,1)} %all-gather.11.cloned.1.call-done, f32[640,1280]{1,0:T(8,128)S(1)} %copy-done.1), kind=kOutput, calls=%fused_computation.42 | convolution fusion | flops 8395161600 | bytes 26222088 | tf_op jit(solution)/shard_map/dot_general | solution.py:11
  518.6 39.6 %all-reduce = (f32[1]{0:T(128)}, f32[1]{0:T(128)}, f32[]{:T(128)}, f32[]{:T(128)}) all-reduce(f32[1]{0:T(128)} %bitcast.1, f32[1]{0:T(128)} %bitcast, f32[]{:T(128)} %get-tuple-element.6, f32[]{:T(128)} %get-tuple-element.4), channel_id=1, replica_groups=mesh['row'=8,'col'=4] {'row','col'}, use_global_device_ids=true, to_apply=%region_5.7 | all-reduce | flops 4 | bytes 32 | tf_op jit(solution)/shard_map/psum | solution.py:54
  559.7 1.8 pad_maximum_fusion
  (2 shorter events, 0.0 us)
Async XLA Ops:
  7.2 164.9 %all-gather.5.cloned.1.call-start = ((), (), s32[]{:S(2)}) async-start(), calls=%async_computation | async-start | bytes 14745600 | tf_op jit(solution)/shard_map/all_gather | solution.py:44
  11.7 248.9 %all-gather.7.cloned.1.call-start = ((), (), s32[]{:S(2)}) async-start(), calls=%async_computation.1 | async-start | bytes 14745600 | tf_op jit(solution)/shard_map/all_gather | solution.py:48
  11.7 41.1 %collective-permute-start = (bf16[640,1280]{1,0:T(8,128)(2,1)}, bf16[640,1280]{1,0:T(8,128)(2,1)S(1)}, u32[]{:S(2)}, u32[]{:S(2)}) collective-permute-start(bf16[640,1280]{1,0:T(8,128)(2,1)} %get-tuple-element.13), channel_id=1, source_target_pairs={{0,1},{1,2},{2,3},{3,0},{4,5},{5,6},{6,7},{7,4},{8,9},{9,10},{10,1... | collective-permute-start | bytes 4915208 | tf_op jit(solution)/shard_map/ppermute | solution.py:29
  52.9 38.8 %collective-permute-start.1 = (bf16[640,1280]{1,0:T(8,128)(2,1)S(1)}, bf16[640,1280]{1,0:T(8,128)(2,1)S(1)}, u32[]{:S(2)}, u32[]{:S(2)}) collective-permute-start(bf16[640,1280]{1,0:T(8,128)(2,1)S(1)} %collective-permute-done), channel_id=1, source_target_pairs={{0,1},{1,2},{2,3},{3,0},{4,5},{5,6},{6,7},{7,4},{8,9},{9,10},{10,1... | collective-permute-start | bytes 4915208 | tf_op jit(solution)/shard_map/ppermute | solution.py:29
  91.6 58.5 %collective-permute-start.2 = (bf16[640,1280]{1,0:T(8,128)(2,1)S(1)}, bf16[640,1280]{1,0:T(8,128)(2,1)}, u32[]{:S(2)}, u32[]{:S(2)}) collective-permute-start(bf16[640,1280]{1,0:T(8,128)(2,1)S(1)} %collective-permute-done.1), channel_id=1, source_target_pairs={{0,1},{1,2},{2,3},{3,0},{4,5},{5,6},{6,7},{7,4},{8,9},{9,10},{10,1... | collective-permute-start | bytes 4915208 | tf_op jit(solution)/shard_map/ppermute | solution.py:29
  172.1 88.5 %copy-start = (bf16[640,1280]{1,0:T(8,128)(2,1)S(1)}, bf16[640,1280]{1,0:T(8,128)(2,1)}, u32[]{:S(2)}) copy-start(bf16[640,1280]{1,0:T(8,128)(2,1)} %get-tuple-element.13) | copy-start | bytes 4915204
  186.2 230.1 %all-gather.9.cloned.1.call-start = ((), (), s32[]{:S(2)}) async-start(), calls=%async_computation.2 | async-start | bytes 14745600 | tf_op jit(solution)/shard_map/all_gather | solution.py:44
  277.5 224.5 %all-gather.11.cloned.1.call-start = ((), (), s32[]{:S(2)}) async-start(), calls=%async_computation.3 | async-start | bytes 14745600 | tf_op jit(solution)/shard_map/all_gather | solution.py:48
  277.6 40.0 %collective-permute-start.3 = (bf16[640,1280]{1,0:T(8,128)(2,1)}, bf16[640,1280]{1,0:T(8,128)(2,1)S(1)}, u32[]{:S(2)}, u32[]{:S(2)}) collective-permute-start(bf16[640,1280]{1,0:T(8,128)(2,1)} %get-tuple-element.14), channel_id=1, source_target_pairs={{0,1},{1,2},{2,3},{3,0},{4,5},{5,6},{6,7},{7,4},{8,9},{9,10},{10,1... | collective-permute-start | bytes 4915208 | tf_op jit(solution)/shard_map/ppermute | solution.py:29
  317.6 38.9 %collective-permute-start.4 = (bf16[640,1280]{1,0:T(8,128)(2,1)S(1)}, bf16[640,1280]{1,0:T(8,128)(2,1)S(1)}, u32[]{:S(2)}, u32[]{:S(2)}) collective-permute-start(bf16[640,1280]{1,0:T(8,128)(2,1)S(1)} %collective-permute-done.3), channel_id=1, source_target_pairs={{0,1},{1,2},{2,3},{3,0},{4,5},{5,6},{6,7},{7,4},{8,9},{9,10},{10,1... | collective-permute-start | bytes 4915208 | tf_op jit(solution)/shard_map/ppermute | solution.py:29
  356.5 38.0 %collective-permute-start.5 = (bf16[640,1280]{1,0:T(8,128)(2,1)S(1)}, bf16[640,1280]{1,0:T(8,128)(2,1)S(1)}, u32[]{:S(2)}, u32[]{:S(2)}) collective-permute-start(bf16[640,1280]{1,0:T(8,128)(2,1)S(1)} %collective-permute-done.4), channel_id=1, source_target_pairs={{0,1},{1,2},{2,3},{3,0},{4,5},{5,6},{6,7},{7,4},{8,9},{9,10},{10,1... | collective-permute-start | bytes 4915208 | tf_op jit(solution)/shard_map/ppermute | solution.py:29
  416.3 85.7 %copy-start.1 = (f32[640,1280]{1,0:T(8,128)S(1)}, f32[640,1280]{1,0:T(8,128)}, u32[]{:S(2)}) copy-start(f32[640,1280]{1,0:T(8,128)} %get-tuple-element.15) | copy-start | bytes 9830404
Sparse Core Ops, SparseCore 0:
  11.8 76.9 all-gather.4
  186.3 74.2 all-gather.6
  277.7 74.1 all-gather.8
  430.6 71.4 all-gather.10
